TPU v7x, 1024 devices: a whole 4x8x16 slice. The times are simulated.
1024 devices in a mesh: outer: 64 (over y_hi, z, core), inner: 16 (over y_lo, x).
Axes of the slice: x: 4, y: 8 (y_hi: 2, y_lo: 4; y = y_hi * 4 + y_lo), z: 16, core: 2. Of those that a mesh axis runs over, the one named last changes fastest.
Arguments:
- queries: bfloat16 [131072, 4096], P(('outer', 'inner')), may hold values from -8 to 8
- keys: bfloat16 [131072, 512], P(('outer', 'inner')), may hold values from -8 to 8
- values: bfloat16 [131072, 512], P(('outer', 'inner')), may hold values from -6 to 6
- acc_out: bfloat16 [131072, 4096], P(('outer', 'inner')), may hold values from -6 to 6
- acc_max: float32 [131072, 32], P(('outer', 'inner')), may hold values from 2 to 4
- acc_sum: float32 [131072, 32], P(('outer', 'inner')), may hold values from 16 to 256
- doc_lengths: int32 [128], replicated, may hold values from 1 to 8192, as said below
Outputs:
- new_out: bfloat16 [131072, 4096], P(('outer', 'inner'))
- new_max: float32 [131072, 32], P(('outer', 'inner'))
- new_sum: float32 [131072, 32], P(('outer', 'inner'))
Inputs may be any that keep to these rules, and one draw needn't show every extreme that they name: `doc_lengths`: the lengths add up to 131072; one document is exactly 8192 long and none is longer.
All inputs are finite; a program needn't handle non-finite values.
Results may differ from a plain program's by a relative error of at most 0.0014.
Values may be sent and summed in bfloat16 or wider, within the bound.
A program may use at most 32 MiB of HBM per device.

v0:
```python
import math

import jax
import jax.numpy as jnp
from jax import lax
from jax.sharding import PartitionSpec as P

HD = 128


NEG = -1e30


def shifted(value, axis, steps):
    count = lax.axis_size(axis)
    initial, last = (max(0, -steps), min(count, count - steps))
    return lax.ppermute(value, axis, [(source, source + steps) for source in range(initial, last)])


def doc_start_of(doc_lengths, positions):
    ends = jnp.cumsum(doc_lengths)
    starts = ends - doc_lengths
    inside = starts[None, :] <= positions[:, None]
    return jnp.max(jnp.where(inside, starts[None, :], 0), axis=1)


def attend_block(carry, q_heads, key_tile, value_tile, kpos, qpos, qstart, scale):
    mask = (kpos[None, :] <= qpos[:, None]) & (kpos[None, :] >= qstart[:, None])

    def live(state):
        run_max, run_sum, run_out = state
        scores = (
            jnp.einsum("rhgd,nhd->rhgn", q_heads, key_tile, preferred_element_type=jnp.float32)
            * scale
        )
        keep = mask[:, None, None, :]
        scores = jnp.where(keep, scores, NEG)
        top = jnp.maximum(run_max, jnp.max(scores, axis=-1))
        shrink = jnp.exp(run_max - top)
        weights = jnp.where(keep, jnp.exp(scores - top[..., None]), 0.0)
        total = run_sum * shrink + jnp.sum(weights, axis=-1)
        mixed = jnp.einsum(
            "rhgn,nhd->rhgd",
            weights.astype(jnp.bfloat16),
            value_tile,
            preferred_element_type=jnp.float32,
        )
        return (top, total, run_out * shrink[..., None] + mixed)

    return lax.cond(jnp.any(mask), live, lambda state: state, carry)


def body(queries, keys, values, acc_out, acc_max, acc_sum, doc_lengths):
    rows = queries.shape[0]
    heads = acc_max.shape[1]
    kv_heads = keys.shape[1] // HD
    group = heads // kv_heads
    n_outer = lax.axis_size("outer")
    n_inner = lax.axis_size("inner")
    block = rows * n_inner
    outer_at = lax.axis_index("outer")
    inner_at = lax.axis_index("inner")
    scale = 1.0 / math.sqrt(HD)
    k_block = (outer_at + n_outer - 1) % n_outer
    key_here, value_here = shifted((keys, values), "outer", 1)
    qpos = outer_at * block + inner_at * rows + jnp.arange(rows, dtype=jnp.int32)
    qstart = doc_start_of(doc_lengths, qpos)
    q_heads = queries.reshape(rows, kv_heads, group, HD)
    start_state = (
        jnp.full((rows, kv_heads, group), NEG, jnp.float32),
        jnp.zeros((rows, kv_heads, group), jnp.float32),
        jnp.zeros((rows, kv_heads, group, HD), jnp.float32),
    )
    carry = start_state
    key_rows = lax.all_gather(key_here, "inner", axis=0, tiled=True)
    value_rows = lax.all_gather(value_here, "inner", axis=0, tiled=True)
    count = key_rows.shape[0]
    width = 512
    number = count // width
    key_tiles = key_rows.reshape(number, width, kv_heads, HD)
    value_tiles = value_rows.reshape(number, width, kv_heads, HD)
    offsets = width * jnp.arange(number, dtype=jnp.int32)

    def one_tile(state, item):
        key_tile, value_tile, first = item
        kpos = k_block * block + first + jnp.arange(width, dtype=jnp.int32)
        return (attend_block(state, q_heads, key_tile, value_tile, kpos, qpos, qstart, scale), None)

    carry, unused = lax.scan(one_tile, carry, (key_tiles, value_tiles, offsets))
    part_max, part_sum, part_out = carry
    old_max = acc_max.reshape(rows, kv_heads, group)
    old_sum = acc_sum.reshape(rows, kv_heads, group)
    top = jnp.maximum(old_max, part_max)
    kept = old_sum * jnp.exp(old_max - top)
    fresh = jnp.exp(part_max - top)
    total = kept + part_sum * fresh
    old_out = acc_out.reshape(rows, kv_heads, group, HD).astype(jnp.float32)
    result = (old_out * kept[..., None] + part_out * fresh[..., None]) / total[..., None]
    return (
        result.reshape(rows, heads * HD).astype(jnp.bfloat16),
        top.reshape(rows, heads),
        total.reshape(rows, heads),
    )


def solution(mesh):
    return jax.shard_map(
        body,
        mesh=mesh,
        in_specs=(
            P(("outer", "inner"), None),
            P(("outer", "inner"), None),
            P(("outer", "inner"), None),
            P(("outer", "inner"), None),
            P(("outer", "inner"), None),
            P(("outer", "inner"), None),
            P(),
        ),
        out_specs=(
            P(("outer", "inner"), None),
            P(("outer", "inner"), None),
            P(("outer", "inner"), None),
        ),
        check_vma=False,
    )
```

profile of v0, /device:TPU:384, one launch (start us, length us, event | category | flops | bytes accessed | tf_op | source)
XLA Modules:
  0.0 271.6 jit_solution(1454495508296882616)
XLA Ops:
  7.2 0.0 all-gather.3.cloned.1.call-start
  7.2 1.9 collective-permute-start
  9.1 4.6 %collective-permute-done = bf16[128,512]{1,0:T(8,128)(2,1)S(1)} collective-permute-done((bf16[128,512]{1,0:T(8,128)(2,1)}, bf16[128,512]{1,0:T(8,128)(2,1)S(1)}, u32[]{:S(2)}, u32[]{:S(2)}) %collective-permute-start) | collective-permute-done | bytes 131104 | tf_op jit(solution)/shard_map/ppermute | solution.py:17
  13.7 0.6 copy-done.4
  14.3 0.0 all-gather.3.cloned.1.call-update
  14.4 0.0 all-gather.5.cloned.1.call-start
  14.4 2.1 collective-permute-start.1
  16.5 4.4 %collective-permute-done.1 = bf16[128,512]{1,0:T(8,128)(2,1)S(1)} collective-permute-done((bf16[128,512]{1,0:T(8,128)(2,1)}, bf16[128,512]{1,0:T(8,128)(2,1)S(1)}, u32[]{:S(2)}, u32[]{:S(2)}) %collective-permute-start.1) | collective-permute-done | bytes 131104 | tf_op jit(solution)/shard_map/ppermute | solution.py:17
  20.9 0.6 copy-done.5
  21.6 0.0 all-gather.5.cloned.1.call-update
  21.6 0.8 copy.24
  22.4 0.2 reduce-window.9
  22.5 0.1 reduce
  22.6 0.7 sub.30
  23.3 1.7 copy.25
  25.0 0.7 copy.27
  25.7 1.3 copy.23
  27.0 0.2 select_reduce_fusion
  27.2 83.4 %all-gather.3.cloned.1.call-done = bf16[2048,512]{1,0:T(8,128)(2,1)} async-done(((bf16[128,512]{1,0:T(8,128)(2,1)}), bf16[2048,512]{1,0:T(8,128)(2,1)}) %all-gather.3.cloned.1.call-update) | async-done | bytes 2097168 | tf_op jit(solution)/shard_map/all_gather | solution.py:75
  110.6 4.0 %reshape.79 = bf16[4,512,4,128]{3,2,1,0:T(4,128)(2,1)} reshape(bf16[2048,512]{1,0:T(8,128)(2,1)} %all-gather.3.cloned.1.call-done) | data formatting | bytes 4194304 | tf_op jit(solution)/shard_map/reshape | solution.py:80
  114.5 2.0 copy.26
  116.5 86.4 %all-gather.5.cloned.1.call-done = bf16[2048,512]{1,0:T(8,128)(2,1)} async-done(((bf16[128,512]{1,0:T(8,128)(2,1)}), bf16[2048,512]{1,0:T(8,128)(2,1)}) %all-gather.5.cloned.1.call-update) | async-done | bytes 2097168 | tf_op jit(solution)/shard_map/all_gather | solution.py:76
  202.9 4.0 %reshape.81 = bf16[4,512,4,128]{3,2,1,0:T(4,128)(2,1)} reshape(bf16[2048,512]{1,0:T(8,128)(2,1)} %all-gather.5.cloned.1.call-done) | data formatting | bytes 4194304 | tf_op jit(solution)/shard_map/reshape | solution.py:81
  206.9 3.4 %copy.28 = bf16[4,512,4,128]{3,1,2,0:T(8,128)(2,1)} copy(bf16[4,512,4,128]{3,2,1,0:T(4,128)(2,1)} %reshape.81) | data formatting | bytes 4194304
  210.3 1.6 broadcast_in_dim.58
  211.8 46.5 %while.17 = (s32[]{:T(128)}, f32[128,4,8]{0,2,1:T(8,128)S(1)}, f32[128,4,8]{0,2,1:T(8,128)S(1)}, f32[128,4,8,128]{3,0,2,1:T(8,128)}, s32[4]{0:T(128)S(1)}, /*ind...) while((s32[]{:T(128)}, f32[128,4,8]{0,2,1:T(8,128)S(1)}, ...), condition=%wide.region_8.9_spmd.clone, body=%wide.region_2.8_spmd.clone.sunk | while | flops 1102324352 | bytes 48765264 | solution.py:89
  211.8 0.6 dynamic_slice.37
  213.1 0.8 compare_and_fusion.2
  214.5 9.0 %conditional.3 = ((f32[128,4,8]{0,2,1:T(8,128)S(1)}, f32[128,4,8]{0,2,1:T(8,128)S(1)}, f32[128,4,8,128]{3,0,2,1:T(8,128)})) conditional(s32[]{:T(128)} %convert_element_type.34, (f32[128,4,8]{0,2,1:T(8,128)S(1)}, f32[128,4,8]{0,2,1:T(8,128)S(1)}, f32[128,4,8,128]{3,0,2,1:T(8,128)}) %tuple.60, (pred[128,512]{0,1:T(8,128)(4,1)S(1)}, ...), branch_computations={%region_4.4_spmd, %region_5.7_spmd} | conditional | flops 1102061568 | bytes 48693852 | solution.py:50
  214.5 1.3 fusion.2
  215.8 0.0 copy-start
  215.8 2.1 fusion.4
  217.9 0.0 copy-done
  218.0 4.2 %bitcast_add_fusion = f32[128,4,8,128]{3,0,2,1:T(8,128)S(1)} fusion(f32[128,4,8,128]{3,0,2,1:T(8,128)S(1)} %copy-done, f32[4,512,128,8]{2,1,3,0:T(8,128)S(1)} %get-tuple-element.298, f32[128,4,8]{0,2,1:T(8,128)S(1)} %max.6, pred[128,512]{0,1:T(8,128)(4,1)S(1)} %get-tuple-element.183, f32[128,4,8]{0,2,1:T(8,128)S(1)} %get-tuple-element.293, ...), kind=kOutput, calls=%fused_computation.8 | convolution fusion | flops 548405248 | bytes 13206016 | tf_op jit(solution)/shard_map/while/body/eval_jaxpr/cond/branch_1_fun/rhgn,nhd->rhgd/dot_general | solution.py:42
  222.1 1.3 copy-done.1
  223.4 0.6 dynamic_slice.37
  224.7 0.8 compare_and_fusion.2
  226.1 9.0 %conditional.3 = ((f32[128,4,8]{0,2,1:T(8,128)S(1)}, f32[128,4,8]{0,2,1:T(8,128)S(1)}, f32[128,4,8,128]{3,0,2,1:T(8,128)})) conditional(s32[]{:T(128)} %convert_element_type.34, (f32[128,4,8]{0,2,1:T(8,128)S(1)}, f32[128,4,8]{0,2,1:T(8,128)S(1)}, f32[128,4,8,128]{3,0,2,1:T(8,128)}) %tuple.60, (pred[128,512]{0,1:T(8,128)(4,1)S(1)}, ...), branch_computations={%region_4.4_spmd, %region_5.7_spmd} | conditional | flops 1102061568 | bytes 48693852 | solution.py:50
  226.1 1.3 fusion.2
  227.4 0.0 copy-start
  227.4 2.1 fusion.4
  229.6 4.2 %bitcast_add_fusion = f32[128,4,8,128]{3,0,2,1:T(8,128)S(1)} fusion(f32[128,4,8,128]{3,0,2,1:T(8,128)S(1)} %copy-done, f32[4,512,128,8]{2,1,3,0:T(8,128)S(1)} %get-tuple-element.298, f32[128,4,8]{0,2,1:T(8,128)S(1)} %max.6, pred[128,512]{0,1:T(8,128)(4,1)S(1)} %get-tuple-element.183, f32[128,4,8]{0,2,1:T(8,128)S(1)} %get-tuple-element.293, ...), kind=kOutput, calls=%fused_computation.8 | convolution fusion | flops 548405248 | bytes 13206016 | tf_op jit(solution)/shard_map/while/body/eval_jaxpr/cond/branch_1_fun/rhgn,nhd->rhgd/dot_general | solution.py:42
  233.8 1.3 copy-done.1
  235.1 0.6 dynamic_slice.37
  236.3 0.8 compare_and_fusion.2
  237.7 9.0 %conditional.3 = ((f32[128,4,8]{0,2,1:T(8,128)S(1)}, f32[128,4,8]{0,2,1:T(8,128)S(1)}, f32[128,4,8,128]{3,0,2,1:T(8,128)})) conditional(s32[]{:T(128)} %convert_element_type.34, (f32[128,4,8]{0,2,1:T(8,128)S(1)}, f32[128,4,8]{0,2,1:T(8,128)S(1)}, f32[128,4,8,128]{3,0,2,1:T(8,128)}) %tuple.60, (pred[128,512]{0,1:T(8,128)(4,1)S(1)}, ...), branch_computations={%region_4.4_spmd, %region_5.7_spmd} | conditional | flops 1102061568 | bytes 48693852 | solution.py:50
  237.7 1.3 fusion.2
  239.0 0.0 copy-start
  239.0 2.1 fusion.4
  241.2 4.2 %bitcast_add_fusion = f32[128,4,8,128]{3,0,2,1:T(8,128)S(1)} fusion(f32[128,4,8,128]{3,0,2,1:T(8,128)S(1)} %copy-done, f32[4,512,128,8]{2,1,3,0:T(8,128)S(1)} %get-tuple-element.298, f32[128,4,8]{0,2,1:T(8,128)S(1)} %max.6, pred[128,512]{0,1:T(8,128)(4,1)S(1)} %get-tuple-element.183, f32[128,4,8]{0,2,1:T(8,128)S(1)} %get-tuple-element.293, ...), kind=kOutput, calls=%fused_computation.8 | convolution fusion | flops 548405248 | bytes 13206016 | tf_op jit(solution)/shard_map/while/body/eval_jaxpr/cond/branch_1_fun/rhgn,nhd->rhgd/dot_general | solution.py:42
  245.4 0.0 copy-start.1
  245.4 1.3 copy-done.1
  246.7 0.6 dynamic_slice.37
  247.9 0.8 compare_and_fusion.2
  249.3 9.0 %conditional.3 = ((f32[128,4,8]{0,2,1:T(8,128)S(1)}, f32[128,4,8]{0,2,1:T(8,128)S(1)}, f32[128,4,8,128]{3,0,2,1:T(8,128)})) conditional(s32[]{:T(128)} %convert_element_type.34, (f32[128,4,8]{0,2,1:T(8,128)S(1)}, f32[128,4,8]{0,2,1:T(8,128)S(1)}, f32[128,4,8,128]{3,0,2,1:T(8,128)}) %tuple.60, (pred[128,512]{0,1:T(8,128)(4,1)S(1)}, ...), branch_computations={%region_4.4_spmd, %region_5.7_spmd} | conditional | flops 1102061568 | bytes 48693852 | solution.py:50
  249.3 1.3 fusion.2
  250.7 0.0 copy-start
  250.7 2.1 fusion.4
  252.8 4.2 %bitcast_add_fusion = f32[128,4,8,128]{3,0,2,1:T(8,128)S(1)} fusion(f32[128,4,8,128]{3,0,2,1:T(8,128)S(1)} %copy-done, f32[4,512,128,8]{2,1,3,0:T(8,128)S(1)} %get-tuple-element.298, f32[128,4,8]{0,2,1:T(8,128)S(1)} %max.6, pred[128,512]{0,1:T(8,128)(4,1)S(1)} %get-tuple-element.183, f32[128,4,8]{0,2,1:T(8,128)S(1)} %get-tuple-element.293, ...), kind=kOutput, calls=%fused_computation.8 | convolution fusion | flops 548405248 | bytes 13206016 | tf_op jit(solution)/shard_map/while/body/eval_jaxpr/cond/branch_1_fun/rhgn,nhd->rhgd/dot_general | solution.py:42
  257.0 1.3 copy-done.1
  258.3 2.0 copy.29
  260.3 0.6 multiply_add_fusion.1
  261.0 1.5 fusion.23
  262.5 2.3 copy.30
  (42 shorter events, 0.2 us)
Async XLA Ops:
  7.2 103.4 %all-gather.3.cloned.1.call-start = ((), (), s32[]{:S(2)}) async-start(), calls=%async_computation | async-start | bytes 2228224 | tf_op jit(solution)/shard_map/all_gather | solution.py:75
  7.2 6.5 %collective-permute-start = (bf16[128,512]{1,0:T(8,128)(2,1)}, bf16[128,512]{1,0:T(8,128)(2,1)S(1)}, u32[]{:S(2)}, u32[]{:S(2)}) collective-permute-start(bf16[128,512]{1,0:T(8,128)(2,1)} %param.12), channel_id=1, source_target_pairs={{0,16},{16,32},{32,48},{48,64},{64,80},{80,96},{96,112},{112,128},... | collective-permute-start | bytes 393224 | tf_op jit(solution)/shard_map/ppermute | solution.py:17
  13.7 0.6 copy-start.4
  14.4 188.6 %all-gather.5.cloned.1.call-start = ((), (), s32[]{:S(2)}) async-start(), calls=%async_computation.1 | async-start | bytes 2228224 | tf_op jit(solution)/shard_map/all_gather | solution.py:76
  14.4 6.5 %collective-permute-start.1 = (bf16[128,512]{1,0:T(8,128)(2,1)}, bf16[128,512]{1,0:T(8,128)(2,1)S(1)}, u32[]{:S(2)}, u32[]{:S(2)}) collective-permute-start(bf16[128,512]{1,0:T(8,128)(2,1)} %param.13), channel_id=1, source_target_pairs={{0,16},{16,32},{32,48},{48,64},{64,80},{80,96},{96,112},{112,128},... | collective-permute-start | bytes 393224 | tf_op jit(solution)/shard_map/ppermute | solution.py:17
  20.9 0.7 copy-start.5
  23.3 2.4 copy-start.3
  215.8 2.2 copy-start
  222.1 1.3 copy-start.1
  227.4 2.2 copy-start
  233.7 1.3 copy-start.1
  239.0 2.2 copy-start
  245.4 1.3 copy-start.1
  250.7 2.2 copy-start
  257.0 1.3 copy-start.1
  258.3 2.0 copy-start.7
  258.3 2.0 copy-start.8
  258.3 2.7 copy-start.2
  261.0 1.5 copy-start.6
Sparse Core Ops, SparseCore 0:
  14.5 96.0 all-gather.2
  113.2 89.6 all-gather.4
where the time goes:
time: 272 us
  waiting for transfers between devices  179 us (66%)
  local copies, waits for them, and re-layouts  32.5 us (12%)
  matrix products  21.8 us (8%)
  other arithmetic  14.9 us (5%)
  between operations  14.2 us (5%)
  loops' own time  5.34 us (2%)
  starting transfers between devices  4.05 us (1%)
    all_gather x1, waiting for transfers between devices, body(): value_rows = lax.all_gather(value_here, 'inner', axis=0, tiled=True)  86.4 us
    all_gather x1, waiting for transfers between devices, body(): key_rows = lax.all_gather(key_here, 'inner', axis=0, tiled=True)  83.4 us
    dot_general x4, matrix products, live(): jnp.einsum('rhgn,nhd->rhgd', weights.astype(jnp.bfloat16), value_tile, pr...  16.6 us
    unnamed x20, local copies, waits for them, and re-layouts  12.6 us
    ppermute x2, waiting for transfers between devices, shifted(): lax.ppermute(value, axis, [(source, source + steps) for source in range(i...  9 us
    reduce_sum x4, other arithmetic, live(): total = run_sum * shrink + jnp.sum(weights, axis=-1)  8.47 us
  transfers between devices with their start and end apart: 4, of which 4 were waited for; matrix products, arithmetic and copies ran while one was open for 4% of the time, Pallas kernels for 0%

commit v1 on v0

v1 whole, which is shorter than its diff:
```python
import functools
import math

import jax
import jax.numpy as jnp
from jax import lax
from jax.experimental import pallas as pl
from jax.experimental.pallas import tpu as pltpu
from jax.sharding import PartitionSpec as P

HD = 128
NEG = -1e30
LOG2E = math.log2(math.e)
MESH = pl.DeviceIdType.MESH
NX = 4
NY = 4


def kernel(
    q_hbm, k_hbm, v_hbm, ao_hbm, am_hbm, as_hbm, dl_hbm,
    o_hbm, nm_hbm, ns_hbm,
    qs, aos, ams, ass, dls, kbuf, vbuf, acc, m_ref, l_ref, bias, thr,
    in_sem, q_sem, recv_sem, z_sem, y_sem, x_sem, f_sem, out_sem,
):
    rows = k_hbm.shape[0]
    kv_heads = k_hbm.shape[1] // HD
    heads = q_hbm.shape[1] // HD
    group = heads // kv_heads
    wide = group * rows
    n_outer = lax.axis_size("outer")
    half_outer = n_outer // 2
    b = lax.axis_index("outer")
    inner = lax.axis_index("inner")
    y = inner // NX
    x = inner % NX
    xr = (x + 1) % NX
    xl = (x + NX - 1) % NX
    xo = (x + 2) % NX
    nxt = (b + 1) % n_outer
    prv = (b + n_outer - 1) % n_outer
    turn_out = nxt % half_outer == 0
    turn_in = b % half_outer == 0
    y_out = jnp.where(turn_out, NY - 1 - y, y)
    y_in = jnp.where(turn_in, NY - 1 - y, y)
    has_up = y < NY - 1
    has_down = y > 0

    loads = [
        pltpu.make_async_copy(dl_hbm, dls, in_sem.at[0]),
        pltpu.make_async_copy(am_hbm, ams, in_sem.at[1]),
        pltpu.make_async_copy(as_hbm, ass, in_sem.at[2]),
        pltpu.make_async_copy(ao_hbm, aos, in_sem.at[3]),
    ]
    for copy in loads:
        copy.start()
    q_loads = []
    for h in range(heads):
        q_loads.append(
            pltpu.make_async_copy(
                q_hbm.at[:, pl.ds(h * HD, HD)],
                qs.at[h // group, pl.ds((h % group) * rows, rows), :],
                q_sem.at[h],
            )
        )
        q_loads[-1].start()

    barrier = pltpu.get_barrier_semaphore()

    def greet(device):
        pl.semaphore_signal(barrier, inc=1, device_id=device, device_id_type=MESH)

    greet((prv, y_in * NX + x))
    greet((b, y * NX + xr))
    greet((b, y * NX + xl))

    @pl.when(has_up)
    def _():
        greet((b, (y + 1) * NX + x))

    @pl.when(has_down)
    def _():
        greet((b, (y - 1) * NX + x))

    pl.semaphore_wait(barrier, 3 + has_up.astype(jnp.int32) + has_down.astype(jnp.int32))

    bufs = (kbuf, vbuf)
    sources = (k_hbm, v_hbm)

    z_copies = [
        pltpu.make_async_remote_copy(
            src_ref=sources[kv],
            dst_ref=bufs[kv].at[x, y_out],
            send_sem=z_sem.at[kv],
            recv_sem=recv_sem.at[kv, x, y_out],
            device_id=(nxt, y_out * NX + x),
            device_id_type=MESH,
        )
        for kv in range(2)
    ]
    for copy in z_copies:
        copy.start()

    def forward(kv, cx, cy, sem, device):
        return pltpu.make_async_remote_copy(
            src_ref=bufs[kv].at[cx, cy],
            dst_ref=bufs[kv].at[cx, cy],
            send_sem=sem,
            recv_sem=recv_sem.at[kv, cx, cy],
            device_id=device,
            device_id_type=MESH,
        )

    def arrived(kv, cx, cy):
        pltpu.make_async_copy(
            bufs[kv].at[cx, cy], bufs[kv].at[cx, cy], recv_sem.at[kv, cx, cy]
        ).wait()

    def pick(values):
        return jnp.where(
            y == 0, values[0], jnp.where(y == 1, values[1], jnp.where(y == 2, values[2], values[3]))
        )

    order = (y, pick((1, 0, 3, 2)), pick((2, 2, 1, 1)), pick((3, 3, 0, 0)))
    pending = []

    def send(copy, when=None):
        if when is None:
            copy.start()
        else:
            pl.when(when)(copy.start)
        pending.append((copy, when))

    def column(o):
        cy = order[o]
        up = has_up & (cy <= y)
        down = has_down & (cy >= y)
        for kv in range(2):
            arrived(kv, x, cy)
            send(forward(kv, x, cy, y_sem.at[kv, o, 0], (b, (y + 1) * NX + x)), up)
            send(forward(kv, x, cy, y_sem.at[kv, o, 1], (b, (y - 1) * NX + x)), down)
            send(forward(kv, x, cy, x_sem.at[kv, o, 0], (b, y * NX + xr)))
            send(forward(kv, x, cy, x_sem.at[kv, o, 1], (b, y * NX + xl)))

    def relay(o):
        cy = order[o]
        arrived(0, xl, cy)
        send(forward(0, xl, cy, f_sem.at[o, 0], (b, y * NX + xr)))
        arrived(1, xr, cy)
        send(forward(1, xr, cy, f_sem.at[o, 1], (b, y * NX + xl)))

    def prepare():
        for copy in loads:
            copy.wait()
        lane = lax.broadcasted_iota(jnp.int32, (8, 128), 1)
        lengths = jnp.broadcast_to(dls[...], (8, 128))
        ends = lengths
        step = 1
        while step < 128:
            ends = ends + jnp.where(lane >= step, pltpu.roll(ends, step, axis=1), 0)
            step *= 2
        starts = (ends - lengths).astype(jnp.float32)
        starts = jnp.broadcast_to(starts[0:1, :], (128, 128)).T
        first = b * rows * NX * NY + inner * rows
        qpos = (first + lax.broadcasted_iota(jnp.int32, (128, 128), 1)).astype(jnp.float32)
        begin = jnp.max(jnp.where(starts <= qpos, starts, 0.0), axis=0, keepdims=True)
        key_first = ((b - 1) * rows * NX * NY).astype(jnp.float32)
        limit = jnp.where(b == 0, jnp.float32(1e9), begin - key_first)
        thr[...] = jnp.broadcast_to(limit, (8, 128))
        for h in range(heads):
            g, j = h // group, h % group
            cols = pl.ds(j * rows, rows)
            m_ref[g, :, cols] = jnp.broadcast_to(ams[h : h + 1, :] * LOG2E, (8, rows))
            total = jnp.broadcast_to(ass[h : h + 1, :], (8, rows))
            l_ref[g, :, cols] = total * 0.125
            old = aos[:, pl.ds(h * HD, HD)].astype(jnp.float32).T
            acc[g, :, cols] = old * ass[h : h + 1, :]

    scale = LOG2E / math.sqrt(HD)

    def unit(cx, first, count):
        keys = count * rows
        for part in range(count):
            cy = first + part
            true_y = jnp.where(turn_in, NY - 1 - cy, cy)
            base = (true_y * NX + cx) * rows
            kpos = (base + lax.broadcasted_iota(jnp.int32, (rows, 128), 0)).astype(jnp.float32)
            bias[pl.ds(part * rows, rows), :] = jnp.where(kpos >= thr[0:1, :], 0.0, NEG)

        def head(g, carry):
            cols = pl.ds(pl.multiple_of(g * HD, HD), HD)
            kt = kbuf[cx, pl.ds(first, count), :, cols].reshape(keys, HD)
            vt = vbuf[cx, pl.ds(first, count), :, cols].reshape(keys, HD).T
            scores, weights, shrinks = {}, {}, {}

            def stage_scores(j):
                scores[j] = lax.dot_general(
                    kt, qs[g, pl.ds(j * rows, rows), :], (((1,), (1,)), ((), ())),
                    preferred_element_type=jnp.float32,
                )

            def stage_softmax(j):
                lanes = pl.ds(j * rows, rows)
                st = scores.pop(j) * scale + bias[pl.ds(0, keys), :]
                old = m_ref[g, :, lanes]
                top = jnp.maximum(old, jnp.max(st, axis=0, keepdims=True))
                shrink = jnp.exp2(old - top)
                p = jnp.exp2(st - top[0:1, :])
                part = jnp.sum(p.reshape(keys // 8, 8, rows), axis=0)
                l_ref[g, :, lanes] = l_ref[g, :, lanes] * shrink + part
                m_ref[g, :, lanes] = top
                weights[j] = p.astype(jnp.bfloat16)
                shrinks[j] = shrink

            def stage_mix(j):
                lanes = pl.ds(j * rows, rows)
                mixed = jnp.dot(vt, weights.pop(j), preferred_element_type=jnp.float32)
                acc[g, :, lanes] = acc[g, :, lanes] * shrinks.pop(j)[0:1, :] + mixed

            for j in range(group + 2):
                if j < group:
                    stage_scores(j)
                if 1 <= j <= group:
                    stage_softmax(j - 1)
                if j >= 2:
                    stage_mix(j - 2)
            return carry

        lax.fori_loop(0, kv_heads, head, 0)

    h0 = y // 2 * 2
    h1 = 2 - h0

    prepare()
    column(0)
    column(1)
    relay(0)
    for copy in q_loads:
        copy.wait()
    unit(x, h0, 2)
    column(2)
    relay(1)
    column(3)
    relay(2)
    unit(x, h1, 2)
    relay(3)
    for o in range(NY):
        arrived(1, xl, order[o])
    unit(xl, 0, NY)
    for o in range(NY):
        arrived(0, xr, order[o])
    unit(xr, 0, NY)
    for o in (0, 1):
        arrived(0, xo, order[o])
        arrived(1, xo, order[o])
    unit(xo, h0, 2)
    for o in (2, 3):
        arrived(0, xo, order[o])
        arrived(1, xo, order[o])
    unit(xo, h1, 2)

    outs = []
    for g in range(kv_heads):
        total = jnp.sum(l_ref[g], axis=0, keepdims=True)
        inverse = 1.0 / total
        for j in range(group):
            h = g * group + j
            cols = pl.ds(j * rows, rows)
            ass[h : h + 1, :] = total[:, j * rows : (j + 1) * rows]
            ams[h : h + 1, :] = m_ref[g, 0:1, cols] * (1.0 / LOG2E)
            done = acc[g, :, cols] * inverse[:, j * rows : (j + 1) * rows]
            aos[:, pl.ds(h * HD, HD)] = done.T.astype(jnp.bfloat16)
        span = pl.ds(g * group * HD, group * HD)
        outs.append(pltpu.make_async_copy(aos.at[:, span], o_hbm.at[:, span], out_sem.at[g]))
        outs[-1].start()
    outs.append(pltpu.make_async_copy(ams, nm_hbm, out_sem.at[kv_heads]))
    outs[-1].start()
    outs.append(pltpu.make_async_copy(ass, ns_hbm, out_sem.at[kv_heads + 1]))
    outs[-1].start()
    for copy in z_copies:
        copy.wait_send()
    for copy, when in pending:
        if when is None:
            copy.wait_send()
        else:
            pl.when(when)(copy.wait_send)
    for copy in outs:
        copy.wait()


def body(queries, keys, values, acc_out, acc_max, acc_sum, doc_lengths):
    rows, width = queries.shape
    heads = acc_max.shape[1]
    kv_heads = keys.shape[1] // HD
    wide = heads // kv_heads * rows
    anywhere = pl.BlockSpec(memory_space=pl.ANY)
    out, top, total = pl.pallas_call(
        kernel,
        out_shape=(
            jax.ShapeDtypeStruct((rows, width), jnp.bfloat16),
            jax.ShapeDtypeStruct((heads, rows), jnp.float32),
            jax.ShapeDtypeStruct((heads, rows), jnp.float32),
        ),
        in_specs=[pl.BlockSpec(memory_space=pltpu.HBM)] * 7,
        out_specs=(anywhere,) * 3,
        scratch_shapes=[
            pltpu.VMEM((kv_heads, wide, HD), jnp.bfloat16),
            pltpu.VMEM((rows, width), jnp.bfloat16),
            pltpu.VMEM((heads, rows), jnp.float32),
            pltpu.VMEM((heads, rows), jnp.float32),
            pltpu.VMEM((1, 128), jnp.int32),
            pltpu.VMEM((NX, NY, rows, kv_heads * HD), jnp.bfloat16),
            pltpu.VMEM((NX, NY, rows, kv_heads * HD), jnp.bfloat16),
            pltpu.VMEM((kv_heads, HD, wide), jnp.float32),
            pltpu.VMEM((kv_heads, 8, wide), jnp.float32),
            pltpu.VMEM((kv_heads, 8, wide), jnp.float32),
            pltpu.VMEM((NY * rows, 128), jnp.float32),
            pltpu.VMEM((8, 128), jnp.float32),
            pltpu.SemaphoreType.DMA((4,)),
            pltpu.SemaphoreType.DMA((heads,)),
            pltpu.SemaphoreType.DMA((2, NX, NY)),
            pltpu.SemaphoreType.DMA((2,)),
            pltpu.SemaphoreType.DMA((2, NY, 2)),
            pltpu.SemaphoreType.DMA((2, NY, 2)),
            pltpu.SemaphoreType.DMA((NY, 2)),
            pltpu.SemaphoreType.DMA((kv_heads + 2,)),
        ],
        compiler_params=pltpu.CompilerParams(
            collective_id=0, has_side_effects=True, vmem_limit_bytes=48 << 20
        ),
        name="gather_attend",
    )(*[pltpu.with_memory_space_constraint(t, pltpu.HBM) for t in (queries, keys, values, acc_out, acc_max.T, acc_sum.T, doc_lengths.reshape(1, -1))])
    return out, top.T, total.T


def solution(mesh):
    spec = P(("outer", "inner"), None)
    return jax.shard_map(
        body,
        mesh=mesh,
        in_specs=(spec,) * 6 + (P(),),
        out_specs=(spec,) * 3,
        check_vma=False,
    )
```

time: 272 us -> 69.7 us (0.26)
  the two profiles are of different devices: /device:TPU:384 before, /device:TPU:4 now
where the time goes in v1:
time: 69.7 us; the launch traced here: 69.5 us
  Pallas kernels  66.7 us (96%)
  local copies, waits for them, and re-layouts  2.18 us (3%)
    pallas_call x1, Pallas kernels, body(): pl.pallas_call(kernel, out_shape=(jax.ShapeDtypeStruct((rows, width), jnp...  66.7 us
    unnamed x3, local copies, waits for them, and re-layouts  2.18 us

profile of v1, /device:TPU:4, one launch (start us, length us, event | category | flops | bytes accessed | tf_op | source)
XLA Modules:
  0.0 69.5 jit_solution(872477214607510775)
XLA Ops:
  0.6 66.7 %gather_attend.1 = (bf16[128,4096]{1,0:T(8,128)(2,1)S(1)}, f32[32,128]{1,0:T(8,128)S(1)}, f32[32,128]{1,0:T(8,128)S(1)}) custom-call(bf16[128,4096]{1,0:T(8,128)(2,1)} %q_hbm.1, bf16[128,512]{1,0:T(8,128)(2,1)} %k_hbm.1, bf16[128,512]{1,0:T(8,128)(2,1)} %v_hbm.1, bf16[128,4096]{1,0:T(8,128)(2,1)} %ao_hbm.1, f32[32,128]{1,0:T(8,128)} %bitcast.7, ...), custom_call_target="tpu_custom_call" | custom-call | tf_op jit(solution)/shard_map/gather_attend/pallas_call | solution.py:296
  67.4 1.0 %copy.13 = bf16[128,4096]{1,0:T(8,128)(2,1)} copy(bf16[128,4096]{1,0:T(8,128)(2,1)S(1)} %get-tuple-element.12) | data formatting | bytes 2097152
  68.3 0.6 copy.14
  68.9 0.6 copy.15

commit v2 on v1

--- a/solution.py
+++ b/solution.py
@@ -18,9 +18,9 @@
 
 def kernel(
     q_hbm, k_hbm, v_hbm, ao_hbm, am_hbm, as_hbm, dl_hbm,
-    o_hbm, nm_hbm, ns_hbm,
+    o_ref, nm_ref, ns_ref,
     qs, aos, ams, ass, dls, kbuf, vbuf, acc, m_ref, l_ref, bias, thr,
-    in_sem, q_sem, recv_sem, z_sem, y_sem, x_sem, f_sem, out_sem,
+    in_sem, q_sem, recv_sem, z_sem, y_sem, x_sem, f_sem,
 ):
     rows = k_hbm.shape[0]
     kv_heads = k_hbm.shape[1] // HD
@@ -44,6 +44,46 @@
     y_in = jnp.where(turn_in, NY - 1 - y, y)
     has_up = y < NY - 1
     has_down = y > 0
+    fed = b > 0
+    feeds = b < n_outer - 1
+
+    barrier = pltpu.get_barrier_semaphore()
+
+    def greet(device):
+        pl.semaphore_signal(barrier, inc=1, device_id=device, device_id_type=MESH)
+
+    def meet():
+        greet((prv, y_in * NX + x))
+        greet((b, y * NX + xr))
+        greet((b, y * NX + xl))
+        pl.when(has_up)(lambda: greet((b, (y + 1) * NX + x)))
+        pl.when(has_down)(lambda: greet((b, (y - 1) * NX + x)))
+
+    pl.when(fed)(meet)
+
+    peers = jnp.where(fed, 2 + has_up.astype(jnp.int32) + has_down.astype(jnp.int32), 0)
+    pl.semaphore_wait(barrier, peers + feeds.astype(jnp.int32))
+
+    bufs = (kbuf, vbuf)
+    sources = (k_hbm, v_hbm)
+
+    z_copies = [
+        pltpu.make_async_remote_copy(
+            src_ref=sources[kv],
+            dst_ref=bufs[kv].at[x, y_out],
+            send_sem=z_sem.at[kv],
+            recv_sem=recv_sem.at[kv, x, y_out],
+            device_id=(nxt, y_out * NX + x),
+            device_id_type=MESH,
+        )
+        for kv in range(2)
+    ]
+
+    def feed():
+        for copy in z_copies:
+            copy.start()
+
+    pl.when(feeds)(feed)
 
     loads = [
         pltpu.make_async_copy(dl_hbm, dls, in_sem.at[0]),
@@ -63,42 +103,6 @@
             )
         )
         q_loads[-1].start()
-
-    barrier = pltpu.get_barrier_semaphore()
-
-    def greet(device):
-        pl.semaphore_signal(barrier, inc=1, device_id=device, device_id_type=MESH)
-
-    greet((prv, y_in * NX + x))
-    greet((b, y * NX + xr))
-    greet((b, y * NX + xl))
-
-    @pl.when(has_up)
-    def _():
-        greet((b, (y + 1) * NX + x))
-
-    @pl.when(has_down)
-    def _():
-        greet((b, (y - 1) * NX + x))
-
-    pl.semaphore_wait(barrier, 3 + has_up.astype(jnp.int32) + has_down.astype(jnp.int32))
-
-    bufs = (kbuf, vbuf)
-    sources = (k_hbm, v_hbm)
-
-    z_copies = [
-        pltpu.make_async_remote_copy(
-            src_ref=sources[kv],
-            dst_ref=bufs[kv].at[x, y_out],
-            send_sem=z_sem.at[kv],
-            recv_sem=recv_sem.at[kv, x, y_out],
-            device_id=(nxt, y_out * NX + x),
-            device_id_type=MESH,
-        )
-        for kv in range(2)
-    ]
-    for copy in z_copies:
-        copy.start()
 
     def forward(kv, cx, cy, sem, device):
         return pltpu.make_async_remote_copy(
@@ -177,19 +181,31 @@
 
     scale = LOG2E / math.sqrt(HD)
 
-    def unit(cx, first, count):
-        keys = count * rows
-        for part in range(count):
-            cy = first + part
-            true_y = jnp.where(turn_in, NY - 1 - cy, cy)
-            base = (true_y * NX + cx) * rows
-            kpos = (base + lax.broadcasted_iota(jnp.int32, (rows, 128), 0)).astype(jnp.float32)
-            bias[pl.ds(part * rows, rows), :] = jnp.where(kpos >= thr[0:1, :], 0.0, NEG)
+    def unit(parts, g_first=0, g_last=None):
+        keys = len(parts) * 2 * rows
+
+        def set_bias():
+            for n, (cx, first) in enumerate(parts):
+                for half in range(2):
+                    cy = first + half
+                    true_y = jnp.where(turn_in, NY - 1 - cy, cy)
+                    base = (true_y * NX + cx) * rows
+                    kpos = base + lax.broadcasted_iota(jnp.int32, (rows, 128), 0)
+                    bias[pl.ds((n * 2 + half) * rows, rows), :] = jnp.where(
+                        kpos.astype(jnp.float32) >= thr[0:1, :], 0.0, NEG
+                    )
+
+        if g_first == 0:
+            set_bias()
+
+        def rows_of(buf, cols):
+            tiles = [buf[cx, pl.ds(first, 2), :, cols].reshape(2 * rows, HD) for cx, first in parts]
+            return tiles[0] if len(tiles) == 1 else jnp.concatenate(tiles, axis=0)
 
         def head(g, carry):
             cols = pl.ds(pl.multiple_of(g * HD, HD), HD)
-            kt = kbuf[cx, pl.ds(first, count), :, cols].reshape(keys, HD)
-            vt = vbuf[cx, pl.ds(first, count), :, cols].reshape(keys, HD).T
+            kt = rows_of(kbuf, cols)
+            vt = rows_of(vbuf, cols).T
             scores, weights, shrinks = {}, {}, {}
 
             def stage_scores(j):
@@ -225,66 +241,73 @@
                     stage_mix(j - 2)
             return carry
 
-        lax.fori_loop(0, kv_heads, head, 0)
-
-    h0 = y // 2 * 2
-    h1 = 2 - h0
+        lax.fori_loop(g_first, kv_heads if g_last is None else g_last, head, 0)
 
     prepare()
-    column(0)
-    column(1)
-    relay(0)
     for copy in q_loads:
         copy.wait()
-    unit(x, h0, 2)
-    column(2)
-    relay(1)
-    column(3)
-    relay(2)
-    unit(x, h1, 2)
-    relay(3)
-    for o in range(NY):
-        arrived(1, xl, order[o])
-    unit(xl, 0, NY)
-    for o in range(NY):
-        arrived(0, xr, order[o])
-    unit(xr, 0, NY)
-    for o in (0, 1):
-        arrived(0, xo, order[o])
-        arrived(1, xo, order[o])
-    unit(xo, h0, 2)
-    for o in (2, 3):
-        arrived(0, xo, order[o])
-        arrived(1, xo, order[o])
-    unit(xo, h1, 2)
-
-    outs = []
+
+    def attend():
+        h0 = y // 2 * 2
+        h1 = 2 - h0
+        column(0)
+        column(1)
+        relay(0)
+        unit([(x, h0)], 0, 1)
+        column(2)
+        unit([(x, h0)], 1, 2)
+        relay(1)
+        unit([(x, h0)], 2, 3)
+        column(3)
+        unit([(x, h0)], 3, 4)
+        arrived(1, xl, order[0])
+        arrived(1, xl, order[1])
+        arrived(0, xr, order[0])
+        arrived(0, xr, order[1])
+        unit([(xl, h0), (xr, h0)], 0, 1)
+        relay(2)
+        unit([(xl, h0), (xr, h0)], 1, 4)
+        arrived(0, xo, order[0])
+        arrived(1, xo, order[0])
+        arrived(0, xo, order[1])
+        arrived(1, xo, order[1])
+        unit([(x, h1), (xo, h0)], 0, 1)
+        relay(3)
+        unit([(x, h1), (xo, h0)], 1, 4)
+        arrived(1, xl, order[2])
+        arrived(1, xl, order[3])
+        arrived(0, xr, order[2])
+        arrived(0, xr, order[3])
+        unit([(xl, h1), (xr, h1)])
+        arrived(0, xo, order[2])
+        arrived(1, xo, order[2])
+        arrived(0, xo, order[3])
+        arrived(1, xo, order[3])
+        unit([(xo, h1)])
+        for copy, when in pending:
+            if when is None:
+                copy.wait_send()
+            else:
+                pl.when(when)(copy.wait_send)
+
+    pl.when(fed)(attend)
+
     for g in range(kv_heads):
         total = jnp.sum(l_ref[g], axis=0, keepdims=True)
         inverse = 1.0 / total
         for j in range(group):
             h = g * group + j
             cols = pl.ds(j * rows, rows)
-            ass[h : h + 1, :] = total[:, j * rows : (j + 1) * rows]
-            ams[h : h + 1, :] = m_ref[g, 0:1, cols] * (1.0 / LOG2E)
+            ns_ref[h : h + 1, :] = total[:, j * rows : (j + 1) * rows]
+            nm_ref[h : h + 1, :] = m_ref[g, 0:1, cols] * (1.0 / LOG2E)
             done = acc[g, :, cols] * inverse[:, j * rows : (j + 1) * rows]
-            aos[:, pl.ds(h * HD, HD)] = done.T.astype(jnp.bfloat16)
-        span = pl.ds(g * group * HD, group * HD)
-        outs.append(pltpu.make_async_copy(aos.at[:, span], o_hbm.at[:, span], out_sem.at[g]))
-        outs[-1].start()
-    outs.append(pltpu.make_async_copy(ams, nm_hbm, out_sem.at[kv_heads]))
-    outs[-1].start()
-    outs.append(pltpu.make_async_copy(ass, ns_hbm, out_sem.at[kv_heads + 1]))
-    outs[-1].start()
-    for copy in z_copies:
-        copy.wait_send()
-    for copy, when in pending:
-        if when is None:
+            o_ref[:, pl.ds(h * HD, HD)] = done.T.astype(jnp.bfloat16)
+
+    def fed_next():
+        for copy in z_copies:
             copy.wait_send()
-        else:
-            pl.when(when)(copy.wait_send)
-    for copy in outs:
-        copy.wait()
+
+    pl.when(feeds)(fed_next)
 
 
 def body(queries, keys, values, acc_out, acc_max, acc_sum, doc_lengths):
@@ -301,7 +324,7 @@
             jax.ShapeDtypeStruct((heads, rows), jnp.float32),
         ),
         in_specs=[pl.BlockSpec(memory_space=pltpu.HBM)] * 7,
-        out_specs=(anywhere,) * 3,
+        out_specs=(pl.BlockSpec(memory_space=pltpu.VMEM),) * 3,
         scratch_shapes=[
             pltpu.VMEM((kv_heads, wide, HD), jnp.bfloat16),
             pltpu.VMEM((rows, width), jnp.bfloat16),
@@ -322,7 +345,6 @@
             pltpu.SemaphoreType.DMA((2, NY, 2)),
             pltpu.SemaphoreType.DMA((2, NY, 2)),
             pltpu.SemaphoreType.DMA((NY, 2)),
-            pltpu.SemaphoreType.DMA((kv_heads + 2,)),
         ],
         compiler_params=pltpu.CompilerParams(
             collective_id=0, has_side_effects=True, vmem_limit_bytes=48 << 20

time: 69.7 us -> 58.7 us (0.84)
  the two profiles are of different devices: /device:TPU:4 before, /device:TPU:38 now
where the time goes in v2:
time: 58.7 us; the launch traced here: 58.5 us
  Pallas kernels  55.7 us (95%)
  local copies, waits for them, and re-layouts  2.18 us (4%)
  between operations  0.64 us (1%)
    pallas_call x1, Pallas kernels, body(): pl.pallas_call(kernel, out_shape=(jax.ShapeDtypeStruct((rows, width), jnp...  55.7 us
    unnamed x3, local copies, waits for them, and re-layouts  2.18 us

profile of v2, /device:TPU:38, one launch (start us, length us, event | category | flops | bytes accessed | tf_op | source)
XLA Modules:
  0.0 58.5 jit_solution(4187491704821659392)
XLA Ops:
  0.6 55.7 %gather_attend.1 = (bf16[128,4096]{1,0:T(8,128)(2,1)S(1)}, f32[32,128]{1,0:T(8,128)S(1)}, f32[32,128]{1,0:T(8,128)S(1)}) custom-call(bf16[128,4096]{1,0:T(8,128)(2,1)} %q_hbm.1, bf16[128,512]{1,0:T(8,128)(2,1)} %k_hbm.1, bf16[128,512]{1,0:T(8,128)(2,1)} %v_hbm.1, bf16[128,4096]{1,0:T(8,128)(2,1)} %ao_hbm.1, f32[32,128]{1,0:T(8,128)} %bitcast.7, ...), custom_call_target="tpu_custom_call" | custom-call | tf_op jit(solution)/shard_map/gather_attend/pallas_call | solution.py:319
  56.3 1.0 %copy.13 = bf16[128,4096]{1,0:T(8,128)(2,1)} copy(bf16[128,4096]{1,0:T(8,128)(2,1)S(1)} %get-tuple-element.12) | data formatting | bytes 2097152
  57.3 0.6 %copy.14 = f32[128,32]{0,1:T(8,128)} copy(f32[128,32]{0,1:T(8,128)S(1)} %bitcast.6) | data formatting | bytes 32768
  57.9 0.6 %copy.15 = f32[128,32]{0,1:T(8,128)} copy(f32[128,32]{0,1:T(8,128)S(1)} %bitcast.5) | data formatting | bytes 32768

commit v3 on v2

--- a/solution.py
+++ b/solution.py
@@ -18,7 +18,7 @@
 
 def kernel(
     q_hbm, k_hbm, v_hbm, ao_hbm, am_hbm, as_hbm, dl_hbm,
-    o_ref, nm_ref, ns_ref,
+    o_ref, st_ref,
     qs, aos, ams, ass, dls, kbuf, vbuf, acc, m_ref, l_ref, bias, thr,
     in_sem, q_sem, recv_sem, z_sem, y_sem, x_sem, f_sem,
 ):
@@ -182,24 +182,26 @@
     scale = LOG2E / math.sqrt(HD)
 
     def unit(parts, g_first=0, g_last=None):
-        keys = len(parts) * 2 * rows
+        keys = sum(count for _, _, count in parts) * rows
 
         def set_bias():
-            for n, (cx, first) in enumerate(parts):
-                for half in range(2):
-                    cy = first + half
-                    true_y = jnp.where(turn_in, NY - 1 - cy, cy)
-                    base = (true_y * NX + cx) * rows
-                    kpos = base + lax.broadcasted_iota(jnp.int32, (rows, 128), 0)
-                    bias[pl.ds((n * 2 + half) * rows, rows), :] = jnp.where(
-                        kpos.astype(jnp.float32) >= thr[0:1, :], 0.0, NEG
-                    )
+            slots = [(cx, first + n) for cx, first, count in parts for n in range(count)]
+            for n, (cx, cy) in enumerate(slots):
+                true_y = jnp.where(turn_in, NY - 1 - cy, cy)
+                base = (true_y * NX + cx) * rows
+                kpos = base + lax.broadcasted_iota(jnp.int32, (rows, 128), 0)
+                bias[pl.ds(n * rows, rows), :] = jnp.where(
+                    kpos.astype(jnp.float32) >= thr[0:1, :], 0.0, NEG
+                )
 
         if g_first == 0:
             set_bias()
 
         def rows_of(buf, cols):
-            tiles = [buf[cx, pl.ds(first, 2), :, cols].reshape(2 * rows, HD) for cx, first in parts]
+            tiles = [
+                buf[cx, pl.ds(first, count), :, cols].reshape(count * rows, HD)
+                for cx, first, count in parts
+            ]
             return tiles[0] if len(tiles) == 1 else jnp.concatenate(tiles, axis=0)
 
         def head(g, carry):
@@ -253,37 +255,37 @@
         column(0)
         column(1)
         relay(0)
-        unit([(x, h0)], 0, 1)
+        unit([(x, h0, 2)], 0, 1)
         column(2)
-        unit([(x, h0)], 1, 2)
+        unit([(x, h0, 2)], 1, 2)
         relay(1)
-        unit([(x, h0)], 2, 3)
+        unit([(x, h0, 2)], 2, 3)
         column(3)
-        unit([(x, h0)], 3, 4)
+        unit([(x, h0, 2)], 3, 4)
         arrived(1, xl, order[0])
         arrived(1, xl, order[1])
         arrived(0, xr, order[0])
         arrived(0, xr, order[1])
-        unit([(xl, h0), (xr, h0)], 0, 1)
+        unit([(xl, h0, 2), (xr, h0, 2)], 0, 2)
         relay(2)
-        unit([(xl, h0), (xr, h0)], 1, 4)
+        unit([(xl, h0, 2), (xr, h0, 2)], 2, 4)
         arrived(0, xo, order[0])
         arrived(1, xo, order[0])
         arrived(0, xo, order[1])
         arrived(1, xo, order[1])
-        unit([(x, h1), (xo, h0)], 0, 1)
+        unit([(x, h1, 2), (xo, h0, 2)], 0, 2)
         relay(3)
-        unit([(x, h1), (xo, h0)], 1, 4)
+        unit([(x, h1, 2), (xo, h0, 2)], 2, 4)
         arrived(1, xl, order[2])
         arrived(1, xl, order[3])
         arrived(0, xr, order[2])
         arrived(0, xr, order[3])
-        unit([(xl, h1), (xr, h1)])
+        unit([(xl, h1, 2), (xr, h1, 2)])
         arrived(0, xo, order[2])
         arrived(1, xo, order[2])
         arrived(0, xo, order[3])
         arrived(1, xo, order[3])
-        unit([(xo, h1)])
+        unit([(xo, h1, 2)])
         for copy, when in pending:
             if when is None:
                 copy.wait_send()
@@ -298,8 +300,8 @@
         for j in range(group):
             h = g * group + j
             cols = pl.ds(j * rows, rows)
-            ns_ref[h : h + 1, :] = total[:, j * rows : (j + 1) * rows]
-            nm_ref[h : h + 1, :] = m_ref[g, 0:1, cols] * (1.0 / LOG2E)
+            st_ref[heads + h : heads + h + 1, :] = total[:, j * rows : (j + 1) * rows]
+            st_ref[h : h + 1, :] = m_ref[g, 0:1, cols] * (1.0 / LOG2E)
             done = acc[g, :, cols] * inverse[:, j * rows : (j + 1) * rows]
             o_ref[:, pl.ds(h * HD, HD)] = done.T.astype(jnp.bfloat16)
 
@@ -316,15 +318,14 @@
     kv_heads = keys.shape[1] // HD
     wide = heads // kv_heads * rows
     anywhere = pl.BlockSpec(memory_space=pl.ANY)
-    out, top, total = pl.pallas_call(
+    out, stats = pl.pallas_call(
         kernel,
         out_shape=(
             jax.ShapeDtypeStruct((rows, width), jnp.bfloat16),
-            jax.ShapeDtypeStruct((heads, rows), jnp.float32),
-            jax.ShapeDtypeStruct((heads, rows), jnp.float32),
+            jax.ShapeDtypeStruct((2 * heads, rows), jnp.float32),
         ),
         in_specs=[pl.BlockSpec(memory_space=pltpu.HBM)] * 7,
-        out_specs=(pl.BlockSpec(memory_space=pltpu.VMEM),) * 3,
+        out_specs=(pl.BlockSpec(memory_space=pltpu.VMEM),) * 2,
         scratch_shapes=[
             pltpu.VMEM((kv_heads, wide, HD), jnp.bfloat16),
             pltpu.VMEM((rows, width), jnp.bfloat16),
@@ -351,7 +352,7 @@
         ),
         name="gather_attend",
     )(*[pltpu.with_memory_space_constraint(t, pltpu.HBM) for t in (queries, keys, values, acc_out, acc_max.T, acc_sum.T, doc_lengths.reshape(1, -1))])
-    return out, top.T, total.T
+    return out, stats[:heads].T, stats[heads:].T
 
 
 def solution(mesh):

time: 58.7 us -> 58.2 us (level)
  local copies, waits for them, and re-layouts: 2.18 us -> 1.58 us
    unnamed x3 -> x1, local copies, waits for them, and re-layouts: 2.18 us -> 0.97 us
    transpose x0 -> x1, local copies, waits for them, and re-layouts: none -> 0.61 us  [body(): return (out, stats[:heads].T, stats[heads:].T)]
where the time goes in v3:
time: 58.2 us; the launch traced here: 58 us
  Pallas kernels  55.8 us (96%)
  local copies, waits for them, and re-layouts  1.58 us (3%)
  between operations  0.64 us (1%)
    pallas_call x1, Pallas kernels, body(): pl.pallas_call(kernel, out_shape=(jax.ShapeDtypeStruct((rows, width), jnp...  55.8 us

profile of v3, /device:TPU:38, one launch (start us, length us, event | category | flops | bytes accessed | tf_op | source)
XLA Modules:
  0.0 58.0 jit_solution(17128468224513138171)
XLA Ops:
  0.6 55.8 %gather_attend.1 = (bf16[128,4096]{1,0:T(8,128)(2,1)S(1)}, f32[64,128]{1,0:T(8,128)S(1)}) custom-call(bf16[128,4096]{1,0:T(8,128)(2,1)} %q_hbm.1, bf16[128,512]{1,0:T(8,128)(2,1)} %k_hbm.1, bf16[128,512]{1,0:T(8,128)(2,1)} %v_hbm.1, bf16[128,4096]{1,0:T(8,128)(2,1)} %ao_hbm.1, f32[32,128]{1,0:T(8,128)} %bitcast.7, f32[32,128]{1,0:T(8,128)} %bitcast.8, ...), custom_call_target="tpu_custom_call" | custom-call | tf_op jit(solution)/shard_map/gather_attend/pallas_call | solution.py:321
  56.4 0.6 %slice_bitcast_fusion = (f32[128,32]{0,1:T(8,128)}, f32[128,32]{0,1:T(8,128)}) fusion(f32[64,128]{1,0:T(8,128)S(1)} %get-tuple-element.6), kind=kLoop, calls=%fused_computation | loop fusion | bytes 65536 | tf_op jit(solution)/shard_map/transpose | solution.py:355
  57.1 1.0 %copy.11 = bf16[128,4096]{1,0:T(8,128)(2,1)} copy(bf16[128,4096]{1,0:T(8,128)(2,1)S(1)} %get-tuple-element.12) | data formatting | bytes 2097152
